TPU v7x, 128 devices: a whole 4x4x4 slice. The times are simulated.
128 devices in a mesh: tm: 8 (over x, z_lo), dp: 16 (over z_hi, y, core).
Axes of the slice: x: 4, y: 4, z: 4 (z_hi: 2, z_lo: 2; z = z_hi * 2 + z_lo), core: 2. Of those that a mesh axis runs over, the one named last changes fastest.
Arguments:
- clips: bfloat16 [16, 32, 32, 64, 128], P('dp', 'tm'), may hold values from -6 to 6
- weight: bfloat16 [3, 3, 3, 128, 256], replicated, may hold values from -0.109375 to 0.109375
- bias: float32 [256], replicated, may hold values from -3 to 3
- out_grad: bfloat16 [16, 16, 16, 32, 256], P('dp', 'tm'), may hold values from -6 to 6
Outputs:
- features: bfloat16 [16, 16, 16, 32, 256], P('dp', 'tm')
- clips_grad: bfloat16 [16, 32, 32, 64, 128], P('dp', 'tm')
- weight_grad: float32 [3, 3, 3, 128, 256], replicated
- bias_grad: float32 [256], replicated
All inputs are finite; a program needn't handle non-finite values.
Results may differ from a plain program's by a relative error of at most 0.005.
Values may be sent and summed in bfloat16 or wider, within the bound.
No kernel may reach another device: no remote copies, remote signals or barrier semaphores. Data moves between devices by JAX's collectives and lax.ppermute only.
A program may use at most 64 MiB of HBM per device.

v0:
```python
import itertools
import math

import jax
import jax.numpy as jnp
from jax import lax
from jax.experimental import pallas as pl
from jax.experimental.pallas import tpu as pltpu
from jax.sharding import PartitionSpec as P

BF = jnp.bfloat16
F32 = jnp.float32
AXES = ("tm", "dp")
MIB = 1 << 20


def device_index(x, y, z, core):
    return (x * 2 + z % 2) * 16 + (z // 2) * 8 + y * 2 + core


PLACES = list(itertools.product(range(4), range(4), range(4), range(2)))
CORE_SWAP = [
    (device_index(x, y, z, c), device_index(x, y, z, 1 - c)) for x, y, z, c in PLACES
]
SAME_CORE = [[device_index(*q) for q in PLACES if q[3] == c] for c in range(2)]


def dot(a, b, ca, cb):
    return lax.dot_general(a, b, (((ca,), (cb,)), ((), ())), preferred_element_type=F32)


def patches_of(x_ref, frame, stage, p_ref, slot):
    zeros = jnp.zeros((8, 128), F32)
    for s in range(4):
        stage[s, 0:8, :] = zeros
    p_ref[slot, 0:32, 0:384] = jnp.zeros((32, 384), BF)

    def step(k, carry):
        for s in range(4):
            stage[s, 8:72, :] = x_ref[0, frame, 4 * k + s].astype(F32)
        for s in range(4):
            taps = [stage[s, pl.ds(7 + j, 32, stride=2), :].astype(BF) for j in range(3)]
            half = 2 * k + s // 2
            here = pl.ds(pl.multiple_of(half * 32, 32), 32)
            below = pl.ds(pl.multiple_of(half * 32 + 32, 32), 32)
            for j in range(3):
                if s % 2 == 0:
                    p_ref[slot, here, 384 + 128 * j : 512 + 128 * j] = taps[j]
                else:
                    p_ref[slot, here, 768 + 128 * j : 896 + 128 * j] = taps[j]
                    p_ref[slot, below, 128 * j : 128 * j + 128] = taps[j]
        return carry

    lax.fori_loop(0, 8, step, 0)


def head_kernel(x_ref, w_ref, p_ref, s_ref, stage):
    for slot in range(2):
        patches_of(x_ref, 2 + slot, stage, p_ref, slot)
    s_ref[...] = (
        dot(p_ref[0, 0:512], w_ref[0], 1, 0) + dot(p_ref[1, 0:512], w_ref[1], 1, 0)
    ).astype(BF)


def gate(pre, grad):
    sig = jax.nn.sigmoid(pre)
    return pre * sig, grad * (sig * (1.0 + pre * (1.0 - sig)))


def body_kernel(x_ref, w_ref, b_ref, g_ref, q_ref, p_ref, feat_ref, pg_ref, pre_ref, dw_ref, stage):
    for slot in range(2):
        patches_of(x_ref, slot, stage, p_ref, slot)
    bias = b_ref[...]
    pre = (
        dot(p_ref[0, 0:512], w_ref[0], 1, 0)
        + dot(p_ref[1, 0:512], w_ref[1], 1, 0)
        + dot(q_ref[0, 0:512], w_ref[2], 1, 0)
        + bias
    )
    feat, grad = gate(pre, g_ref[0, 1].reshape(512, 256).astype(F32))
    feat_ref[...] = feat.astype(BF)
    pg_ref[...] = grad.astype(BF)
    pre_ref[...] = dot(p_ref[0, 0:512], w_ref[2], 1, 0) + bias
    dw_ref[0] = dot(p_ref[0, 0:512], pg_ref[...], 0, 0)
    dw_ref[1] = dot(p_ref[1, 0:512], pg_ref[...], 0, 0)
    dw_ref[2] = dot(q_ref[0, 0:512], pg_ref[...], 0, 0)


def first_kernel(pre_ref, s_ref, g_ref, f1_ref, feat_ref, pg_ref):
    feat, grad = gate(pre_ref[...] + s_ref[...].astype(F32), g_ref[0, 0].reshape(512, 256).astype(F32))
    feat_ref[0, 0] = feat.astype(BF).reshape(16, 32, 256)
    feat_ref[0, 1] = f1_ref[...].reshape(16, 32, 256)
    pg_ref[...] = grad.astype(BF)


def middle_kernel(p_ref, pg0_ref, dw_ref, out_ref):
    out_ref[...] = dw_ref[2] + dot(p_ref[0, 0:512], pg0_ref[...], 0, 0)


def weight_kernel(core_ref, q_ref, pn_ref, pg0_ref, pg1_ref, dw_ref, dw2_ref, out_ref):
    core = core_ref[0]

    def put(rows, value):
        value = value.astype(BF)
        out_ref[core, rows, :] = value[:, 0:128]
        out_ref[1 - core, rows, :] = value[:, 128:256]

    put(slice(2304, 3456), dw2_ref[...])
    for kt in range(2):
        put(
            slice(1152 * kt, 1152 * kt + 1152),
            dw_ref[kt] + dot(q_ref[kt, 0:512], pn_ref[...], 0, 0),
        )
    total = jnp.sum(pg0_ref[...].astype(F32) + pg1_ref[...].astype(F32), axis=0, keepdims=True)
    put(slice(3456, 3584), jnp.broadcast_to(total, (128, 256)))


def back_kernel(w_ref, pg0_ref, pg1_ref, pn_ref, out_ref, pgs, even, odd, stage):
    last = lax.broadcasted_iota(jnp.int32, (512, 256), 0) % 32 == 31
    for k, ref in enumerate((pg0_ref, pg1_ref, pn_ref)):
        here = ref[...]
        pgs[k, 0, 0:512] = here
        moved = jnp.where(last, 0.0, pltpu.roll(here.astype(F32), 511, 0))
        pgs[k, 1, 0:512] = moved.astype(BF)
        pgs[k, 0, 512:544] = jnp.zeros((32, 256), BF)
        pgs[k, 1, 512:544] = jnp.zeros((32, 256), BF)
    sources = (((0, 2), (1, 0)), ((1, 1),), ((1, 2), (2, 0)), ((2, 1),))
    for frame, terms in enumerate(sources):
        for n, (k, kt) in enumerate(terms):
            def rows(kh, kw, count):
                start = 384 * kh + 128 * kw
                return w_ref[kt, start : start + 128 * count, :]

            e = dot(pgs[k, 0, 0:512], rows(1, 1, 2), 1, 1)
            o = dot(pgs[k, 0, 0:512], rows(2, 1, 2), 1, 1) + dot(pgs[k, 0, 32:544], rows(0, 1, 2), 1, 1)
            es = dot(pgs[k, 1, 0:512], rows(1, 0, 1), 1, 1)
            os = dot(pgs[k, 1, 0:512], rows(2, 0, 1), 1, 1) + dot(pgs[k, 1, 32:544], rows(0, 0, 1), 1, 1)
            if n == 0:
                even[...] = e
                odd[...] = o
            else:
                even[...] += e
                odd[...] += o
            even[:, 128:256] += es
            odd[:, 128:256] += os

        def step(h, carry):
            here = pl.ds(pl.multiple_of(h * 32, 32), 32)
            for s, acc in enumerate((even, odd)):
                stage[s, pl.ds(0, 32, stride=2), :] = acc[here, 0:128]
                stage[s, pl.ds(1, 32, stride=2), :] = acc[here, 128:256]
            for s in range(2):
                out_ref[0, frame, 2 * h + s] = stage[s, 0:64, :].astype(BF)
            return carry

        lax.fori_loop(0, 16, step, 0)


VM = pl.BlockSpec(memory_space=pltpu.VMEM)
SM = pl.BlockSpec(memory_space=pltpu.SMEM)


def call(kernel, name, outs, scratch, limit, flops, specs):
    moved = sum(math.prod(s) * d.dtype.itemsize for s, d in ((o.shape, o) for o in outs))
    return pl.pallas_call(
        kernel,
        name=name,
        out_shape=outs if len(outs) > 1 else outs[0],
        in_specs=specs,
        out_specs=[VM] * len(outs) if len(outs) > 1 else VM,
        scratch_shapes=scratch,
        compiler_params=pltpu.CompilerParams(vmem_limit_bytes=limit * MIB),
        cost_estimate=pl.CostEstimate(flops=flops, bytes_accessed=2 * moved, transcendentals=0),
    )


def shape(*dims, dtype=BF):
    return jax.ShapeDtypeStruct(dims, dtype)


def passed_along(value, steps):
    count = lax.axis_size("tm")
    first, last = (max(0, -steps), min(count, count - steps))
    return lax.ppermute(value, "tm", [(source, source + steps) for source in range(first, last)])


def local(clips, weight, bias, out_grad):
    w = weight.reshape(3, 1152, 256)
    unit = 2 * 512 * 1152 * 256
    stage = pltpu.VMEM((4, 72, 128), F32)
    q, part = call(
        head_kernel, "head", [shape(2, 544, 1152), shape(512, 256)], [stage], 8, 2 * unit, [VM] * 2
    )(clips, w)
    prior = passed_along(part, 1)
    p, feat1, pg1, pre0, dw = call(
        body_kernel,
        "body",
        [
            shape(2, 544, 1152),
            shape(512, 256),
            shape(512, 256),
            shape(512, 256, dtype=F32),
            shape(3, 1152, 256, dtype=F32),
        ],
        [stage],
        16,
        7 * unit,
        [VM] * 5,
    )(clips, w, bias.reshape(1, 256), out_grad, q)
    features, pg0 = call(
        first_kernel, "first", [shape(1, 2, 16, 32, 256), shape(512, 256)], [], 8, unit // 10, [VM] * 4
    )(pre0, prior, out_grad, feat1)
    after = passed_along(pg0, -1)
    dw2 = call(middle_kernel, "middle", [shape(1152, 256, dtype=F32)], [], 8, unit, [VM] * 3)(p, pg0, dw)
    core = (lax.axis_index("dp") % 2).astype(jnp.int32).reshape(1)
    halves = call(
        weight_kernel, "weight", [shape(2, 3584, 128)], [], 8, 2 * unit, [SM] + [VM] * 6
    )(core, q, after, pg0, pg1, dw, dw2)
    got = lax.ppermute(halves[1], AXES, CORE_SWAP)
    mine = (halves[0].astype(F32) + got.astype(F32)).astype(BF)
    spread = lax.all_to_all(
        mine.reshape(64, 56, 128), AXES, split_axis=0, concat_axis=0, tiled=True, axis_index_groups=SAME_CORE
    )
    clips_grad = call(
        back_kernel,
        "back",
        [shape(1, 4, 32, 64, 128)],
        [
            pltpu.VMEM((3, 2, 544, 256), BF),
            pltpu.VMEM((512, 256), F32),
            pltpu.VMEM((512, 256), F32),
            pltpu.VMEM((2, 64, 128), F32),
        ],
        16,
        8 * unit,
        [VM] * 4,
    )(w, pg0, pg1, after)
    scale = 1.0 / math.sqrt(1024 * lax.axis_size("tm") * lax.axis_size("dp"))
    own = (jnp.sum(spread.astype(F32), axis=0) * scale).astype(BF)
    whole = lax.all_to_all(
        jnp.broadcast_to(own[None], (64, 56, 128)),
        AXES,
        split_axis=0,
        concat_axis=0,
        tiled=True,
        axis_index_groups=SAME_CORE,
    ).reshape(3584, 128)
    other = lax.ppermute(whole, AXES, CORE_SWAP)
    low = jnp.where(core[0] == 0, whole, other)
    high = jnp.where(core[0] == 0, other, whole)
    sums = jnp.concatenate([low, high], axis=1).astype(F32)
    return features, clips_grad, sums[:3456].reshape(3, 3, 3, 128, 256), sums[3456]


def solution(mesh):
    in_specs = (P("dp", "tm", None, None, None), P(), P(), P("dp", "tm", None, None, None))
    out_specs = (P("dp", "tm", None, None, None), P("dp", "tm", None, None, None), P(), P())
    return jax.shard_map(local, mesh=mesh, in_specs=in_specs, out_specs=out_specs, check_vma=False)
```

profile of v0, /device:TPU:1, one launch (start us, length us, event | category | flops | bytes accessed | tf_op | source)
XLA Modules:
  0.0 93.1 jit_solution(6213547142873496775)
XLA Ops:
  0.6 0.0 copy-start.12
  0.6 0.0 copy-start.4
  0.7 1.6 %copy-done.4 = bf16[1,4,32,64,128]{4,3,2,1,0:T(8,128)(2,1)S(1)} copy-done((bf16[1,4,32,64,128]{4,3,2,1,0:T(8,128)(2,1)S(1)}, bf16[1,4,32,64,128]{4,3,2,1,0:T(8,128)(2,1)}, u32[]{:S(2)}) %copy-start.4) | copy-done | bytes 2097176
  2.2 1.5 %copy-done.6 = bf16[3,3,3,128,256]{4,3,2,1,0:T(8,128)(2,1)S(1)} copy-done((bf16[3,3,3,128,256]{4,3,2,1,0:T(8,128)(2,1)S(1)}, bf16[3,3,3,128,256]{4,3,2,1,0:T(8,128)(2,1)}, u32[]{:S(2)}) %copy-start.6) | copy-done | bytes 1769496
  3.7 1.4 %head.1 = (bf16[2,544,1152]{2,1,0:T(8,128)(2,1)S(1)}, bf16[512,256]{1,0:T(8,128)(2,1)S(1)}) custom-call(bf16[1,4,32,64,128]{4,3,2,1,0:T(8,128)(2,1)S(1)} %copy-done.4, bf16[3,1152,256]{2,1,0:T(8,128)(2,1)S(1)} %bitcast.16), custom_call_target="tpu_custom_call" | custom-call | flops 603979776 | bytes 5537792 | tf_op jit(solution)/shard_map/head/pallas_call | solution.py:191
  5.1 0.0 copy-start
  5.1 4.4 %collective-permute-start = (bf16[512,256]{1,0:T(8,128)(2,1)S(1)}, bf16[512,256]{1,0:T(8,128)(2,1)S(1)}, u32[]{:S(2)}, u32[]{:S(2)}) collective-permute-start(bf16[512,256]{1,0:T(8,128)(2,1)S(1)} %get-tuple-element.15), channel_id=1, source_target_pairs={{0,16},{16,32},{32,48},{48,64},{64,80},{80,96},{96,112},{1,17},{17... | collective-permute-start | bytes 786440 | tf_op jit(solution)/shard_map/ppermute | solution.py:184
  9.5 0.0 copy-done.12
  9.5 4.5 %body.1 = (bf16[2,544,1152]{2,1,0:T(8,128)(2,1)S(1)}, bf16[512,256]{1,0:T(8,128)(2,1)S(1)}, bf16[512,256]{1,0:T(8,128)(2,1)S(1)}, f32[512,256]{1,0:T(8,128)S(1)}, f32[3,1152,256]{2,1,0:T(8,128)S(1)}) custom-call(bf16[1,4,32,64,128]{4,3,2,1,0:T(8,128)(2,1)S(1)} %copy-done.5, bf16[3,1152,256]{2,1,0:T(8,128)(2,1)S(1)} %bitcast.17, f32[1,256]{1,0:T(1,128)S(1)} %bitcast.19, ...), custom_call_target="tpu_custom_call" | custom-call | flops 2113929216 | bytes 14188544 | tf_op jit(solution)/shard_map/body/pallas_call | solution.py:195
  14.0 1.5 %copy-done.2 = bf16[2,544,1152]{2,1,0:T(8,128)(2,1)} copy-done((bf16[2,544,1152]{2,1,0:T(8,128)(2,1)}, bf16[2,544,1152]{2,1,0:T(8,128)(2,1)S(1)}, u32[]{:S(2)}) %copy-start.2) | copy-done | bytes 2506776
  15.5 0.0 collective-permute-done.s_ref
  15.5 1.0 %first.1 = (bf16[1,2,16,32,256]{4,3,2,1,0:T(8,128)(2,1)}, bf16[512,256]{1,0:T(8,128)(2,1)}) custom-call(f32[512,256]{1,0:T(8,128)S(1)} %get-tuple-element.14.pre_ref, bf16[512,256]{1,0:T(8,128)(2,1)S(1)} %collective-permute-done.s_ref, bf16[1,2,16,32,256]{4,3,2,1,0:T(8,128)(2,1)S(1)} %copy-done.8, bf16[512,256]{1,0:T(8,128)(2,1)S(1)} %get-tuple-element.16.f1_ref), custom_call_target="tpu_custom_call" | custom-call | flops 30198988 | bytes 1572864 | tf_op jit(solution)/shard_map/first/pallas_call | solution.py:210
  16.5 1.3 %collective-permute-start.1 = (bf16[512,256]{1,0:T(8,128)(2,1)}, bf16[512,256]{1,0:T(8,128)(2,1)}, u32[]{:S(2)}, u32[]{:S(2)}) collective-permute-start(bf16[512,256]{1,0:T(8,128)(2,1)} %get-tuple-element.18.pg0_ref), channel_id=1, source_target_pairs={{16,0},{32,16},{48,32},{64,48},{80,64},{96,80},{112,96},{17,1},{33... | collective-permute-start | bytes 786440 | tf_op jit(solution)/shard_map/ppermute | solution.py:184
  17.8 1.7 %copy-done.3 = bf16[2,544,1152]{2,1,0:T(8,128)(2,1)S(1)} copy-done((bf16[2,544,1152]{2,1,0:T(8,128)(2,1)S(1)}, bf16[2,544,1152]{2,1,0:T(8,128)(2,1)}, u32[]{:S(2)}) %copy-start.3) | copy-done | bytes 2506776
  19.5 1.6 %middle.1.dw2_ref = f32[1152,256]{1,0:T(8,128)S(1)} custom-call(bf16[2,544,1152]{2,1,0:T(8,128)(2,1)S(1)} %copy-done.3, bf16[512,256]{1,0:T(8,128)(2,1)} %get-tuple-element.18.pg0_ref, f32[3,1152,256]{2,1,0:T(8,128)S(1)} %get-tuple-element.20.dw_ref), custom_call_target="tpu_custom_call" | custom-call | flops 301989888 | bytes 2359296 | tf_op jit(solution)/shard_map/middle/pallas_call | solution.py:214
  21.2 4.5 %collective-permute-done.1.pn_ref = bf16[512,256]{1,0:T(8,128)(2,1)} collective-permute-done((bf16[512,256]{1,0:T(8,128)(2,1)}, bf16[512,256]{1,0:T(8,128)(2,1)}, u32[]{:S(2)}, u32[]{:S(2)}) %collective-permute-start.1) | collective-permute-done | bytes 262176 | tf_op jit(solution)/shard_map/ppermute | solution.py:184
  25.6 2.0 %weight.1 = bf16[2,3584,128]{2,1,0:T(8,128)(2,1)S(1)} custom-call(s32[1]{0:T(128)} %bitcast.2.core_ref, bf16[2,544,1152]{2,1,0:T(8,128)(2,1)S(1)} %copy-done.1, bf16[512,256]{1,0:T(8,128)(2,1)} %collective-permute-done.1.pn_ref, bf16[512,256]{1,0:T(8,128)(2,1)} %get-tuple-element.18.pg0_ref, bf16[512,256]{1,0:T(8,128)(2,1)S(1)} %copy-done.10, ...), custom_call_target="tpu_custom_call" | custom-call | flops 603979776 | bytes 3670016 | tf_op jit(solution)/shard_map/weight/pallas_call | solution.py:216
  27.6 0.1 slice_bitcast_fusion
  27.7 1.9 %collective-permute-start.2 = (bf16[3584,128]{1,0:T(8,128)(2,1)S(1)}, bf16[3584,128]{1,0:T(8,128)(2,1)S(1)}, u32[]{:S(2)}, u32[]{:S(2)}) collective-permute-start(bf16[3584,128]{1,0:T(8,128)(2,1)S(1)} %slice_bitcast_fusion), channel_id=1, source_target_pairs={{0,1},{1,0},{16,17},{17,16},{8,9},{9,8},{24,25},{25,24},{2,3},{3,2... | collective-permute-start | bytes 2752520 | tf_op jit(solution)/shard_map/ppermute | solution.py:219
  29.6 2.1 %collective-permute-done.2 = bf16[3584,128]{1,0:T(8,128)(2,1)S(1)} collective-permute-done((bf16[3584,128]{1,0:T(8,128)(2,1)S(1)}, bf16[3584,128]{1,0:T(8,128)(2,1)S(1)}, u32[]{:S(2)}, u32[]{:S(2)}) %collective-permute-start.2) | collective-permute-done | bytes 917536 | tf_op jit(solution)/shard_map/ppermute | solution.py:219
  31.7 0.2 fusion
  31.9 27.0 %all_to_all.10 = bf16[64,56,128]{2,1,0:T(8,128)(2,1)S(1)} all-to-all(bf16[64,56,128]{2,1,0:T(8,128)(2,1)S(1)} %bitcast.21), channel_id=1, replica_groups={{0,16,8,24,2,18,10,26,4,20,12,28,6,22,14,30,32,48,40,56,34,50,42,58,36,..., dimensions={0} | all-to-all | bytes 1835008 | tf_op jit(solution)/shard_map/all_to_all | solution.py:221
  59.0 0.2 convert_reduce_fusion
  59.1 0.1 broadcast_in_dim.2
  59.3 20.2 %all_to_all.11 = bf16[64,56,128]{2,1,0:T(8,128)(2,1)S(1)} all-to-all(bf16[64,56,128]{2,1,0:T(8,128)(2,1)S(1)} %broadcast_in_dim.2), channel_id=1, replica_groups={{0,16,8,24,2,18,10,26,4,20,12,28,6,22,14,30,32,48,40,56,34,50,42,58,36,..., dimensions={0} | all-to-all | bytes 1835008 | tf_op jit(solution)/shard_map/all_to_all | solution.py:240
  79.4 3.1 %collective-permute-start.3 = (bf16[3584,128]{1,0:T(8,128)(2,1)S(1)}, bf16[3584,128]{1,0:T(8,128)(2,1)}, u32[]{:S(2)}, u32[]{:S(2)}) collective-permute-start(bf16[3584,128]{1,0:T(8,128)(2,1)S(1)} %bitcast.20), channel_id=1, source_target_pairs={{0,1},{1,0},{16,17},{17,16},{8,9},{9,8},{24,25},{25,24},{2,3},{3,2... | collective-permute-start | bytes 2752520 | tf_op jit(solution)/shard_map/ppermute | solution.py:248
  82.6 6.4 %back.1 = bf16[1,4,32,64,128]{4,3,2,1,0:T(8,128)(2,1)} custom-call(bf16[3,1152,256]{2,1,0:T(8,128)(2,1)S(1)} %bitcast.18, bf16[512,256]{1,0:T(8,128)(2,1)} %get-tuple-element.18.pg0_ref, bf16[512,256]{1,0:T(8,128)(2,1)S(1)} %copy-done.11, bf16[512,256]{1,0:T(8,128)(2,1)} %collective-permute-done.1.pn_ref), custom_call_target="tpu_custom_call" | custom-call | flops 2415919104 | bytes 4194304 | tf_op jit(solution)/shard_map/back/pallas_call | solution.py:224
  88.9 0.0 collective-permute-done.3
  88.9 1.3 %broadcast_select_fusion.1 = (bf16[3584,128]{1,0:T(8,128)(2,1)S(1)}, bf16[3584,128]{1,0:T(8,128)(2,1)S(1)}) fusion(bf16[3584,128]{1,0:T(8,128)(2,1)} %collective-permute-done.3, pred[]{:T(512)S(6)} %eq.6, bf16[64,56,128]{2,1,0:T(8,128)(2,1)S(1)} %all_to_all.11), kind=kLoop, calls=%fused_computation.7 | loop fusion | flops 917504 | bytes 3670017 | tf_op jit(solution)/shard_map/jit(_where)/select_n | solution.py:249
  90.2 0.6 maximum_convert_fusion.1
  90.8 0.2 maximum_convert_fusion
  91.1 2.0 %slice.18 = f32[3456,256]{1,0:T(8,128)} slice(f32[3584,256]{1,0:T(8,128)S(1)} %maximum_convert_fusion), slice={[0:3456], [0:256]} | slice | bytes 7077888 | tf_op jit(solution)/shard_map/slice | solution.py:252
  (19 shorter events, 0.0 us)
Async XLA Ops:
  0.6 8.9 %copy-start.12 = (f32[256]{0:T(256)S(1)}, f32[256]{0:T(256)}, u32[]{:S(2)}) copy-start(f32[256]{0:T(256)} %param.6) | copy-start | bytes 3076
  0.6 1.6 %copy-start.4 = (bf16[1,4,32,64,128]{4,3,2,1,0:T(8,128)(2,1)S(1)}, bf16[1,4,32,64,128]{4,3,2,1,0:T(8,128)(2,1)}, u32[]{:S(2)}) copy-start(bf16[1,4,32,64,128]{4,3,2,1,0:T(8,128)(2,1)} %x_ref.3) | copy-start | bytes 6291460
  2.2 1.5 %copy-start.6 = (bf16[3,3,3,128,256]{4,3,2,1,0:T(8,128)(2,1)S(1)}, bf16[3,3,3,128,256]{4,3,2,1,0:T(8,128)(2,1)}, u32[]{:S(2)}) copy-start(bf16[3,3,3,128,256]{4,3,2,1,0:T(8,128)(2,1)} %param.5) | copy-start | bytes 5308420
  3.7 5.8 %copy-start.5 = (bf16[1,4,32,64,128]{4,3,2,1,0:T(8,128)(2,1)S(1)}, bf16[1,4,32,64,128]{4,3,2,1,0:T(8,128)(2,1)}, u32[]{:S(2)}) copy-start(bf16[1,4,32,64,128]{4,3,2,1,0:T(8,128)(2,1)} %x_ref.3) | copy-start | bytes 6291460
  3.7 5.8 %copy-start.8 = (bf16[1,2,16,32,256]{4,3,2,1,0:T(8,128)(2,1)S(1)}, bf16[1,2,16,32,256]{4,3,2,1,0:T(8,128)(2,1)}, u32[]{:S(2)}) copy-start(bf16[1,2,16,32,256]{4,3,2,1,0:T(8,128)(2,1)} %g_ref.3) | copy-start | bytes 1572868
  5.1 8.9 %copy-start = (bf16[2,544,1152]{2,1,0:T(8,128)(2,1)}, bf16[2,544,1152]{2,1,0:T(8,128)(2,1)S(1)}, u32[]{:S(2)}) copy-start(bf16[2,544,1152]{2,1,0:T(8,128)(2,1)S(1)} %get-tuple-element.13.q_ref) | copy-start | bytes 7520260
  5.1 10.4 %collective-permute-start = (bf16[512,256]{1,0:T(8,128)(2,1)S(1)}, bf16[512,256]{1,0:T(8,128)(2,1)S(1)}, u32[]{:S(2)}, u32[]{:S(2)}) collective-permute-start(bf16[512,256]{1,0:T(8,128)(2,1)S(1)} %get-tuple-element.15), channel_id=1, source_target_pairs={{0,16},{16,32},{32,48},{48,64},{64,80},{80,96},{96,112},{1,17},{17... | collective-permute-start | bytes 786440 | tf_op jit(solution)/shard_map/ppermute | solution.py:184
  14.0 1.5 %copy-start.2 = (bf16[2,544,1152]{2,1,0:T(8,128)(2,1)}, bf16[2,544,1152]{2,1,0:T(8,128)(2,1)S(1)}, u32[]{:S(2)}) copy-start(bf16[2,544,1152]{2,1,0:T(8,128)(2,1)S(1)} %get-tuple-element.21.p_ref) | copy-start | bytes 7520260
  15.5 1.0 %copy-start.9 = (bf16[512,256]{1,0:T(8,128)(2,1)}, bf16[512,256]{1,0:T(8,128)(2,1)S(1)}, u32[]{:S(2)}) copy-start(bf16[512,256]{1,0:T(8,128)(2,1)S(1)} %get-tuple-element.19.pg1_ref) | copy-start | bytes 786436
  16.5 9.1 %collective-permute-start.1 = (bf16[512,256]{1,0:T(8,128)(2,1)}, bf16[512,256]{1,0:T(8,128)(2,1)}, u32[]{:S(2)}, u32[]{:S(2)}) collective-permute-start(bf16[512,256]{1,0:T(8,128)(2,1)} %get-tuple-element.18.pg0_ref), channel_id=1, source_target_pairs={{16,0},{32,16},{48,32},{64,48},{80,64},{96,80},{112,96},{17,1},{33... | collective-permute-start | bytes 786440 | tf_op jit(solution)/shard_map/ppermute | solution.py:184
  17.8 1.7 %copy-start.3 = (bf16[2,544,1152]{2,1,0:T(8,128)(2,1)S(1)}, bf16[2,544,1152]{2,1,0:T(8,128)(2,1)}, u32[]{:S(2)}) copy-start(bf16[2,544,1152]{2,1,0:T(8,128)(2,1)} %copy-done.2) | copy-start | bytes 7520260
  19.5 6.1 %copy-start.1 = (bf16[2,544,1152]{2,1,0:T(8,128)(2,1)S(1)}, bf16[2,544,1152]{2,1,0:T(8,128)(2,1)}, u32[]{:S(2)}) copy-start(bf16[2,544,1152]{2,1,0:T(8,128)(2,1)} %copy-done) | copy-start | bytes 7520260
  19.5 6.1 %copy-start.10 = (bf16[512,256]{1,0:T(8,128)(2,1)S(1)}, bf16[512,256]{1,0:T(8,128)(2,1)}, u32[]{:S(2)}) copy-start(bf16[512,256]{1,0:T(8,128)(2,1)} %copy-done.9) | copy-start | bytes 786436
  27.7 4.0 %collective-permute-start.2 = (bf16[3584,128]{1,0:T(8,128)(2,1)S(1)}, bf16[3584,128]{1,0:T(8,128)(2,1)S(1)}, u32[]{:S(2)}, u32[]{:S(2)}) collective-permute-start(bf16[3584,128]{1,0:T(8,128)(2,1)S(1)} %slice_bitcast_fusion), channel_id=1, source_target_pairs={{0,1},{1,0},{16,17},{17,16},{8,9},{9,8},{24,25},{25,24},{2,3},{3,2... | collective-permute-start | bytes 2752520 | tf_op jit(solution)/shard_map/ppermute | solution.py:219
  59.0 23.6 %copy-start.7 = (bf16[3,3,3,128,256]{4,3,2,1,0:T(8,128)(2,1)S(1)}, bf16[3,3,3,128,256]{4,3,2,1,0:T(8,128)(2,1)}, u32[]{:S(2)}) copy-start(bf16[3,3,3,128,256]{4,3,2,1,0:T(8,128)(2,1)} %param.5) | copy-start | bytes 5308420
  59.0 23.6 %copy-start.11 = (bf16[512,256]{1,0:T(8,128)(2,1)S(1)}, bf16[512,256]{1,0:T(8,128)(2,1)}, u32[]{:S(2)}) copy-start(bf16[512,256]{1,0:T(8,128)(2,1)} %copy-done.9) | copy-start | bytes 786436
  79.4 9.5 %collective-permute-start.3 = (bf16[3584,128]{1,0:T(8,128)(2,1)S(1)}, bf16[3584,128]{1,0:T(8,128)(2,1)}, u32[]{:S(2)}, u32[]{:S(2)}) collective-permute-start(bf16[3584,128]{1,0:T(8,128)(2,1)S(1)} %bitcast.20), channel_id=1, source_target_pairs={{0,1},{1,0},{16,17},{17,16},{8,9},{9,8},{24,25},{25,24},{2,3},{3,2... | collective-permute-start | bytes 2752520 | tf_op jit(solution)/shard_map/ppermute | solution.py:248
where the time goes:
time: 93.5 us; the launch traced here: 93.1 us
  blocking collectives  47.2 us (50%)
  Pallas kernels  16.8 us (18%)
  starting transfers between devices  10.7 us (11%)
  local copies, waits for them, and re-layouts  8.48 us (9%)
  waiting for transfers between devices  6.57 us (7%)
  other arithmetic  2.51 us (3%)
    all_to_all x1, blocking collectives, local(): lax.all_to_all(mine.reshape(64, 56, 128), AXES, split_axis=0, concat_axis...  27 us
    all_to_all x1, blocking collectives, local(): lax.all_to_all(jnp.broadcast_to(own[None], (64, 56, 128)), AXES, split_ax...  20.2 us
    pallas_call x1, Pallas kernels, local(): call(back_kernel, 'back', [shape(1, 4, 32, 64, 128)], [pltpu.VMEM((3, 2,...  6.35 us
    unnamed x26, local copies, waits for them, and re-layouts  6.28 us
    ppermute x2, starting transfers between devices, passed_along(): lax.ppermute(value, 'tm', [(source, source + steps) for source in range(f...  5.66 us
    ppermute x2, waiting for transfers between devices, passed_along(): lax.ppermute(value, 'tm', [(source, source + steps) for source in range(f...  4.47 us
    pallas_call x1, Pallas kernels, local(): call(body_kernel, 'body', [shape(2, 544, 1152), shape(512, 256), shape(51...  4.47 us
    ppermute x1, starting transfers between devices, local(): other = lax.ppermute(whole, AXES, CORE_SWAP)  3.14 us
  transfers between devices with their start and end apart: 4, of which 2 were waited for; matrix products, arithmetic and copies ran while one was open for 0% of the time, Pallas kernels for 13%

commit v1 on v0

--- a/solution.py
+++ b/solution.py
@@ -8,6 +8,7 @@
 from jax.experimental.pallas import tpu as pltpu
 from jax.sharding import PartitionSpec as P
 
+
 BF = jnp.bfloat16
 F32 = jnp.float32
 AXES = ("tm", "dp")
@@ -22,7 +23,15 @@
 CORE_SWAP = [
     (device_index(x, y, z, c), device_index(x, y, z, 1 - c)) for x, y, z, c in PLACES
 ]
-SAME_CORE = [[device_index(*q) for q in PLACES if q[3] == c] for c in range(2)]
+RING = (3, 2, 1, 0)
+ROW_SWAP = [(device_index(x, y, z, c), device_index(x, RING[y], z, c)) for x, y, z, c in PLACES]
+TEAMS = [
+    [device_index(x, y, z, c) for x in range(4) for y in pair for z in range(4)]
+    for pair in ((0, 1), (3, 2))
+    for c in range(2)
+]
+TEAM = len(TEAMS[0])
+SHARE = 3584 // TEAM
 
 
 def dot(a, b, ca, cb):
@@ -54,12 +63,24 @@
     lax.fori_loop(0, 8, step, 0)
 
 
-def head_kernel(x_ref, w_ref, p_ref, s_ref, stage):
+def head_kernel(x_ref, w_ref, s_ref, x, w, stage, patches, sems):
+    copies = []
+    for n, frame in enumerate((2, 3, 0, 1)):
+        copies.append(pltpu.make_async_copy(x_ref.at[0, frame], x.at[0, frame], sems.at[n]))
+    for kt in range(3):
+        copies.append(pltpu.make_async_copy(w_ref.at[kt], w.at[kt], sems.at[4 + kt]))
+    for n in (0, 4, 1, 5, 2, 3, 6):
+        copies[n].start()
     for slot in range(2):
-        patches_of(x_ref, 2 + slot, stage, p_ref, slot)
+        copies[slot].wait()
+        patches_of(x, 2 + slot, stage, patches, slot)
+    for slot in range(2):
+        copies[4 + slot].wait()
     s_ref[...] = (
-        dot(p_ref[0, 0:512], w_ref[0], 1, 0) + dot(p_ref[1, 0:512], w_ref[1], 1, 0)
+        dot(patches[0, 0:512], w[0], 1, 0) + dot(patches[1, 0:512], w[1], 1, 0)
     ).astype(BF)
+    for n in (2, 3, 6):
+        copies[n].wait()
 
 
 def gate(pre, grad):
@@ -67,23 +88,17 @@
     return pre * sig, grad * (sig * (1.0 + pre * (1.0 - sig)))
 
 
-def body_kernel(x_ref, w_ref, b_ref, g_ref, q_ref, p_ref, feat_ref, pg_ref, pre_ref, dw_ref, stage):
-    for slot in range(2):
-        patches_of(x_ref, slot, stage, p_ref, slot)
+def body_kernel(x_ref, w_ref, b_ref, g_ref, feat_ref, pg_ref, pre_ref, stage, patches):
+    for slot in range(3):
+        patches_of(x_ref, slot, stage, patches, slot)
     bias = b_ref[...]
-    pre = (
-        dot(p_ref[0, 0:512], w_ref[0], 1, 0)
-        + dot(p_ref[1, 0:512], w_ref[1], 1, 0)
-        + dot(q_ref[0, 0:512], w_ref[2], 1, 0)
-        + bias
-    )
+    pre_ref[...] = dot(patches[0, 0:512], w_ref[2], 1, 0) + bias
+    pre = bias
+    for slot in range(3):
+        pre = pre + dot(patches[slot, 0:512], w_ref[slot], 1, 0)
     feat, grad = gate(pre, g_ref[0, 1].reshape(512, 256).astype(F32))
     feat_ref[...] = feat.astype(BF)
     pg_ref[...] = grad.astype(BF)
-    pre_ref[...] = dot(p_ref[0, 0:512], w_ref[2], 1, 0) + bias
-    dw_ref[0] = dot(p_ref[0, 0:512], pg_ref[...], 0, 0)
-    dw_ref[1] = dot(p_ref[1, 0:512], pg_ref[...], 0, 0)
-    dw_ref[2] = dot(q_ref[0, 0:512], pg_ref[...], 0, 0)
 
 
 def first_kernel(pre_ref, s_ref, g_ref, f1_ref, feat_ref, pg_ref):
@@ -93,11 +108,16 @@
     pg_ref[...] = grad.astype(BF)
 
 
-def middle_kernel(p_ref, pg0_ref, dw_ref, out_ref):
-    out_ref[...] = dw_ref[2] + dot(p_ref[0, 0:512], pg0_ref[...], 0, 0)
-
-
-def weight_kernel(core_ref, q_ref, pn_ref, pg0_ref, pg1_ref, dw_ref, dw2_ref, out_ref):
+def middle_kernel(x_ref, pg0_ref, pg1_ref, q_ref, dw_ref, stage, patches):
+    for slot in range(2):
+        patches_of(x_ref, slot, stage, patches, slot)
+        patches_of(x_ref, 2 + slot, stage, q_ref, slot)
+    dw_ref[0] = dot(patches[0, 0:512], pg1_ref[...], 0, 0)
+    dw_ref[1] = dot(patches[1, 0:512], pg1_ref[...], 0, 0)
+    dw_ref[2] = dot(q_ref[0, 0:512], pg1_ref[...], 0, 0) + dot(patches[0, 0:512], pg0_ref[...], 0, 0)
+
+
+def weight_kernel(core_ref, q_ref, pn_ref, pg0_ref, pg1_ref, dw_ref, out_ref):
     core = core_ref[0]
 
     def put(rows, value):
@@ -105,7 +125,7 @@
         out_ref[core, rows, :] = value[:, 0:128]
         out_ref[1 - core, rows, :] = value[:, 128:256]
 
-    put(slice(2304, 3456), dw2_ref[...])
+    put(slice(2304, 3456), dw_ref[2])
     for kt in range(2):
         put(
             slice(1152 * kt, 1152 * kt + 1152),
@@ -113,6 +133,31 @@
         )
     total = jnp.sum(pg0_ref[...].astype(F32) + pg1_ref[...].astype(F32), axis=0, keepdims=True)
     put(slice(3456, 3584), jnp.broadcast_to(total, (128, 256)))
+
+
+def put_half(half, src_ref, out_ref, wide, sems):
+    copies = []
+    for n in range(4):
+        rows = slice(864 * n, 864 * n + 864)
+        wide[rows, :] = src_ref[rows, :].astype(F32)
+        there = out_ref.at[pl.ds(864 * n, 864), pl.ds(pl.multiple_of(half * 128, 128), 128)]
+        copies.append(pltpu.make_async_copy(wide.at[rows, :], there, sems.at[n]))
+        copies[n].start()
+    for copy in copies:
+        copy.wait()
+
+
+def own_kernel(core_ref, own_ref, out_ref, wide, sems):
+    put_half(core_ref[0], own_ref, out_ref, wide, sems)
+
+
+def other_kernel(core_ref, own_ref, other_ref, held_ref, out_ref, bias_ref, wide, sems):
+    own = own_ref[3456:3464, :].astype(F32)[0:1]
+    other = other_ref[3456:3464, :].astype(F32)[0:1]
+    first = core_ref[0] == 0
+    bias_ref[:, 0:128] = jnp.where(first, own, other)
+    bias_ref[:, 128:256] = jnp.where(first, other, own)
+    put_half(1 - core_ref[0], other_ref, out_ref, wide, sems)
 
 
 def back_kernel(w_ref, pg0_ref, pg1_ref, pn_ref, out_ref, pgs, even, odd, stage):
@@ -157,14 +202,14 @@
 
 
 VM = pl.BlockSpec(memory_space=pltpu.VMEM)
+HB = pl.BlockSpec(memory_space=pltpu.HBM)
 SM = pl.BlockSpec(memory_space=pltpu.SMEM)
 
 
-def call(kernel, name, outs, scratch, limit, flops, specs):
+def call(kernel, outs, scratch, limit, flops, specs):
     moved = sum(math.prod(s) * d.dtype.itemsize for s, d in ((o.shape, o) for o in outs))
     return pl.pallas_call(
         kernel,
-        name=name,
         out_shape=outs if len(outs) > 1 else outs[0],
         in_specs=specs,
         out_specs=[VM] * len(outs) if len(outs) > 1 else VM,
@@ -178,52 +223,88 @@
     return jax.ShapeDtypeStruct(dims, dtype)
 
 
+def in_hbm(value):
+    return pltpu.with_memory_space_constraint(value, pltpu.HBM)
+
+
 def passed_along(value, steps):
     count = lax.axis_size("tm")
     first, last = (max(0, -steps), min(count, count - steps))
     return lax.ppermute(value, "tm", [(source, source + steps) for source in range(first, last)])
 
 
+def spread_over(value):
+    return lax.all_to_all(
+        value, AXES, split_axis=0, concat_axis=0, tiled=True, axis_index_groups=TEAMS
+    )
+
+
+def finish(core, own, other):
+    params = pltpu.CompilerParams(vmem_limit_bytes=8 * MIB)
+    cost = pl.CostEstimate(flops=1 << 20, bytes_accessed=3 * MIB, transcendentals=0)
+    scratch = [pltpu.VMEM((3456, 128), F32), pltpu.SemaphoreType.DMA((4,))]
+    held = pl.pallas_call(
+        own_kernel,
+        name="own",
+        out_shape=shape(3456, 256, dtype=F32),
+        in_specs=[SM, VM],
+        out_specs=HB,
+        scratch_shapes=scratch,
+        compiler_params=params,
+        cost_estimate=cost,
+    )(core, own)
+    return pl.pallas_call(
+        other_kernel,
+        name="other",
+        out_shape=[shape(3456, 256, dtype=F32), shape(1, 256, dtype=F32)],
+        in_specs=[SM, VM, VM, HB],
+        out_specs=[HB, VM],
+        scratch_shapes=scratch,
+        input_output_aliases={3: 0},
+        compiler_params=params,
+        cost_estimate=cost,
+    )(core, own, other, held)
+
+
 def local(clips, weight, bias, out_grad):
-    w = weight.reshape(3, 1152, 256)
     unit = 2 * 512 * 1152 * 256
     stage = pltpu.VMEM((4, 72, 128), F32)
-    q, part = call(
-        head_kernel, "head", [shape(2, 544, 1152), shape(512, 256)], [stage], 8, 2 * unit, [VM] * 2
-    )(clips, w)
+    part, x, w = call(
+        head_kernel,
+        [pltpu.VMEM((512, 256), BF), pltpu.VMEM((1, 4, 32, 64, 128), BF), pltpu.VMEM((3, 1152, 256), BF)],
+        [stage, pltpu.VMEM((2, 544, 1152), BF), pltpu.SemaphoreType.DMA((7,))],
+        16,
+        2 * unit,
+        [HB] * 2,
+    )(in_hbm(clips), in_hbm(weight.reshape(3, 1152, 256)))
     prior = passed_along(part, 1)
-    p, feat1, pg1, pre0, dw = call(
+    feat1, pg1, pre0 = call(
         body_kernel,
-        "body",
-        [
-            shape(2, 544, 1152),
-            shape(512, 256),
-            shape(512, 256),
-            shape(512, 256, dtype=F32),
-            shape(3, 1152, 256, dtype=F32),
-        ],
-        [stage],
+        [shape(512, 256), shape(512, 256), shape(512, 256, dtype=F32)],
+        [stage, pltpu.VMEM((3, 544, 1152), BF)],
         16,
-        7 * unit,
-        [VM] * 5,
-    )(clips, w, bias.reshape(1, 256), out_grad, q)
+        4 * unit,
+        [VM] * 4,
+    )(x, w, bias.reshape(1, 256), out_grad)
     features, pg0 = call(
-        first_kernel, "first", [shape(1, 2, 16, 32, 256), shape(512, 256)], [], 8, unit // 10, [VM] * 4
+        first_kernel, [shape(1, 2, 16, 32, 256), shape(512, 256)], [], 8, unit // 10, [VM] * 4
     )(pre0, prior, out_grad, feat1)
     after = passed_along(pg0, -1)
-    dw2 = call(middle_kernel, "middle", [shape(1152, 256, dtype=F32)], [], 8, unit, [VM] * 3)(p, pg0, dw)
+    q, dw = call(
+        middle_kernel,
+        [shape(2, 544, 1152), shape(3, 1152, 256, dtype=F32)],
+        [stage, pltpu.VMEM((2, 544, 1152), BF)],
+        16,
+        4 * unit,
+        [VM] * 3,
+    )(x, pg0, pg1)
     core = (lax.axis_index("dp") % 2).astype(jnp.int32).reshape(1)
-    halves = call(
-        weight_kernel, "weight", [shape(2, 3584, 128)], [], 8, 2 * unit, [SM] + [VM] * 6
-    )(core, q, after, pg0, pg1, dw, dw2)
+    halves = call(weight_kernel, [shape(2, 3584, 128)], [], 8, 2 * unit, [SM] + [VM] * 5)(core, q, after, pg0, pg1, dw)
     got = lax.ppermute(halves[1], AXES, CORE_SWAP)
     mine = (halves[0].astype(F32) + got.astype(F32)).astype(BF)
-    spread = lax.all_to_all(
-        mine.reshape(64, 56, 128), AXES, split_axis=0, concat_axis=0, tiled=True, axis_index_groups=SAME_CORE
-    )
+    pieces = spread_over(mine.reshape(TEAM, SHARE, 128))
     clips_grad = call(
         back_kernel,
-        "back",
         [shape(1, 4, 32, 64, 128)],
         [
             pltpu.VMEM((3, 2, 544, 256), BF),
@@ -235,21 +316,14 @@
         8 * unit,
         [VM] * 4,
     )(w, pg0, pg1, after)
-    scale = 1.0 / math.sqrt(1024 * lax.axis_size("tm") * lax.axis_size("dp"))
-    own = (jnp.sum(spread.astype(F32), axis=0) * scale).astype(BF)
-    whole = lax.all_to_all(
-        jnp.broadcast_to(own[None], (64, 56, 128)),
-        AXES,
-        split_axis=0,
-        concat_axis=0,
-        tiled=True,
-        axis_index_groups=SAME_CORE,
-    ).reshape(3584, 128)
-    other = lax.ppermute(whole, AXES, CORE_SWAP)
-    low = jnp.where(core[0] == 0, whole, other)
-    high = jnp.where(core[0] == 0, other, whole)
-    sums = jnp.concatenate([low, high], axis=1).astype(F32)
-    return features, clips_grad, sums[:3456].reshape(3, 3, 3, 128, 256), sums[3456]
+    positions = 1024 * lax.axis_size("tm") * lax.axis_size("dp")
+    total = jnp.sum(pieces.astype(F32), axis=0)
+    total = total + lax.ppermute(total, AXES, ROW_SWAP)
+    total = (total * (1.0 / math.sqrt(positions))).astype(BF)
+    own = spread_over(jnp.broadcast_to(total[None], (TEAM, SHARE, 128))).reshape(3584, 128)
+    other = lax.ppermute(own, AXES, CORE_SWAP)
+    weight_grad, bias_grad = finish(core, own, other)
+    return features, clips_grad, weight_grad.reshape(3, 3, 3, 128, 256), bias_grad.reshape(256)
 
 
 def solution(mesh):

time: 93.5 us -> 85.4 us (0.913)
  blocking collectives: 47.2 us -> 38.7 us
  local copies, waits for them, and re-layouts: 8.48 us -> 0.2 us
  waiting for transfers between devices: 6.57 us -> 12.4 us
  starting transfers between devices: 10.7 us -> 14.9 us
  other arithmetic: 2.51 us -> 0.39 us
  Pallas kernels: 16.8 us -> 17.8 us
    all_to_all x2, blocking collectives: 47.2 us -> 38.7 us  [spread_over(): lax.all_to_all(value, AXES, split_axis=0, concat_axis=0, tiled=True, axis...]
    unnamed x26 -> x8, local copies, waits for them, and re-layouts: 6.28 us -> 0.02 us
    ppermute x1 -> x2, starting transfers between devices: 3.14 us -> 7.08 us  [the longest x1 5.13 us: local(): other = lax.ppermute(own, AXES, CORE_SWAP)]
    ppermute x2, waiting for transfers between devices: 4.47 us -> 7.93 us  [passed_along(): lax.ppermute(value, 'tm', [(source, source + steps) for source in range(f...]
    ppermute x1 -> x2, waiting for transfers between devices: 0.01 us -> 2.36 us  [the longest x1 2.36 us: local(): total = total + lax.ppermute(total, AXES, ROW_SWAP)]
    slice x1 -> x0, local copies, waits for them, and re-layouts: 2.02 us -> none  [local(): sums[:3456].reshape(3, 3, 3, 128, 256)]
    select_n x1 -> x0, other arithmetic: 1.3 us -> none  [local(): low = jnp.where(core[0] == 0, whole, other)]
    pallas_call x6 -> x8, Pallas kernels: 16.8 us -> 17.8 us  [the longest x1 5.32 us: local(): call(back_kernel, [shape(1, 4, 32, 64, 128)], [pltpu.VMEM((3, 2, 544, 256...]
  transfers between devices with their start and end apart: 4 -> 5, of which waited for: 2 -> 4; matrix products, arithmetic and copies ran while one was open for 0% -> 0% of each run, Pallas kernels for 13% -> 13%
where the time goes in v1:
time: 85.4 us; the launch traced here: 85.2 us
  blocking collectives  38.7 us (45%)
  Pallas kernels  17.8 us (21%)
  starting transfers between devices  14.9 us (17%)
  waiting for transfers between devices  12.4 us (15%)
    all_to_all x2, blocking collectives, spread_over(): lax.all_to_all(value, AXES, split_axis=0, concat_axis=0, tiled=True, axis...  38.7 us
    ppermute x2, waiting for transfers between devices, passed_along(): lax.ppermute(value, 'tm', [(source, source + steps) for source in range(f...  7.93 us
    ppermute x2, starting transfers between devices, passed_along(): lax.ppermute(value, 'tm', [(source, source + steps) for source in range(f...  5.66 us
    pallas_call x1, Pallas kernels, local(): call(back_kernel, [shape(1, 4, 32, 64, 128)], [pltpu.VMEM((3, 2, 544, 256...  5.32 us
    ppermute x1, starting transfers between devices, local(): other = lax.ppermute(own, AXES, CORE_SWAP)  5.13 us
    pallas_call x1, Pallas kernels, local(): call(head_kernel, [pltpu.VMEM((512, 256), BF), pltpu.VMEM((1, 4, 32, 64,...  2.6 us
    pallas_call x1, Pallas kernels, local(): call(middle_kernel, [shape(2, 544, 1152), shape(3, 1152, 256, dtype=F32)]...  2.51 us
    pallas_call x1, Pallas kernels, local(): call(body_kernel, [shape(512, 256), shape(512, 256), shape(512, 256, dtyp...  2.41 us
  transfers between devices with their start and end apart: 5, of which 4 were waited for; matrix products, arithmetic and copies ran while one was open for 0% of the time, Pallas kernels for 13%

profile of v1, /device:TPU:1, one launch (start us, length us, event | category | flops | bytes accessed | tf_op | source)
XLA Modules:
  0.0 85.2 jit_solution(7992640212556447968)
XLA Ops:
  0.6 0.0 copy-start
  0.6 0.0 copy-start.3
  0.7 2.6 %shard_map.75 = (bf16[512,256]{1,0:T(8,128)(2,1)S(1)}, bf16[1,4,32,64,128]{4,3,2,1,0:T(8,128)(2,1)S(1)}, bf16[3,1152,256]{2,1,0:T(8,128)(2,1)S(1)}) custom-call(bf16[1,4,32,64,128]{4,3,2,1,0:T(8,128)(2,1)} %x_ref.1, bf16[3,1152,256]{2,1,0:T(8,128)(2,1)} %bitcast.20), custom_call_target="tpu_custom_call" | custom-call | flops 603979776 | bytes 8257536 | tf_op jit(solution)/shard_map/pallas_call | solution.py:272
  3.3 0.0 copy-start.1
  3.3 4.4 %collective-permute-start = (bf16[512,256]{1,0:T(8,128)(2,1)S(1)}, bf16[512,256]{1,0:T(8,128)(2,1)S(1)}, u32[]{:S(2)}, u32[]{:S(2)}) collective-permute-start(bf16[512,256]{1,0:T(8,128)(2,1)S(1)} %get-tuple-element.19), channel_id=1, source_target_pairs={{0,16},{16,32},{32,48},{48,64},{64,80},{80,96},{96,112},{1,17},{17... | collective-permute-start | bytes 786440 | tf_op jit(solution)/shard_map/ppermute | solution.py:233
  7.7 0.0 copy-done
  7.7 0.0 copy-done.3
  7.7 2.4 %shard_map.76 = (bf16[512,256]{1,0:T(8,128)(2,1)S(1)}, bf16[512,256]{1,0:T(8,128)(2,1)S(1)}, f32[512,256]{1,0:T(8,128)S(1)}) custom-call(bf16[1,4,32,64,128]{4,3,2,1,0:T(8,128)(2,1)S(1)} %get-tuple-element.16.x_ref, bf16[3,1152,256]{2,1,0:T(8,128)(2,1)S(1)} %get-tuple-element.17.w_ref, f32[1,256]{1,0:T(1,128)S(1)} %bitcast.17, ...), custom_call_target="tpu_custom_call" | custom-call | flops 1207959552 | bytes 2097152 | tf_op jit(solution)/shard_map/pallas_call | solution.py:281
  10.1 0.0 copy-done.1
  10.1 2.5 %collective-permute-done.s_ref = bf16[512,256]{1,0:T(8,128)(2,1)S(1)} collective-permute-done((bf16[512,256]{1,0:T(8,128)(2,1)S(1)}, bf16[512,256]{1,0:T(8,128)(2,1)S(1)}, u32[]{:S(2)}, u32[]{:S(2)}) %collective-permute-start) | collective-permute-done | bytes 262176 | tf_op jit(solution)/shard_map/ppermute | solution.py:233
  12.6 0.9 %shard_map.77 = (bf16[1,2,16,32,256]{4,3,2,1,0:T(8,128)(2,1)}, bf16[512,256]{1,0:T(8,128)(2,1)S(1)}) custom-call(f32[512,256]{1,0:T(8,128)S(1)} %get-tuple-element.18.pre_ref, bf16[512,256]{1,0:T(8,128)(2,1)S(1)} %collective-permute-done.s_ref, bf16[1,2,16,32,256]{4,3,2,1,0:T(8,128)(2,1)S(1)} %copy-done, bf16[512,256]{1,0:T(8,128)(2,1)S(1)} %get-tuple-element.20.f1_ref), custom_call_target="tpu_custom_call" | custom-call | flops 30198988 | bytes 1572864 | tf_op jit(solution)/shard_map/pallas_call | solution.py:289
  13.5 1.3 %collective-permute-start.1 = (bf16[512,256]{1,0:T(8,128)(2,1)S(1)}, bf16[512,256]{1,0:T(8,128)(2,1)S(1)}, u32[]{:S(2)}, u32[]{:S(2)}) collective-permute-start(bf16[512,256]{1,0:T(8,128)(2,1)S(1)} %get-tuple-element.22.pg0_ref), channel_id=1, source_target_pairs={{16,0},{32,16},{48,32},{64,48},{80,64},{96,80},{112,96},{17,1},{33... | collective-permute-start | bytes 786440 | tf_op jit(solution)/shard_map/ppermute | solution.py:233
  14.8 2.5 %shard_map.79 = (bf16[2,544,1152]{2,1,0:T(8,128)(2,1)S(1)}, f32[3,1152,256]{2,1,0:T(8,128)S(1)}) custom-call(bf16[1,4,32,64,128]{4,3,2,1,0:T(8,128)(2,1)S(1)} %get-tuple-element.16.x_ref, bf16[512,256]{1,0:T(8,128)(2,1)S(1)} %get-tuple-element.22.pg0_ref, bf16[512,256]{1,0:T(8,128)(2,1)S(1)} %get-tuple-element.23.pg1_ref), custom_call_target="tpu_custom_call" | custom-call | flops 1207959552 | bytes 12091392 | tf_op jit(solution)/shard_map/pallas_call | solution.py:293
  17.3 5.4 %collective-permute-done.1.pn_ref = bf16[512,256]{1,0:T(8,128)(2,1)S(1)} collective-permute-done((bf16[512,256]{1,0:T(8,128)(2,1)S(1)}, bf16[512,256]{1,0:T(8,128)(2,1)S(1)}, u32[]{:S(2)}, u32[]{:S(2)}) %collective-permute-start.1) | collective-permute-done | bytes 262176 | tf_op jit(solution)/shard_map/ppermute | solution.py:233
  22.8 1.0 %shard_map.80 = bf16[2,3584,128]{2,1,0:T(8,128)(2,1)S(1)} custom-call(s32[1]{0:T(128)} %bitcast.2.core_ref, bf16[2,544,1152]{2,1,0:T(8,128)(2,1)S(1)} %get-tuple-element.24.q_ref, bf16[512,256]{1,0:T(8,128)(2,1)S(1)} %collective-permute-done.1.pn_ref, bf16[512,256]{1,0:T(8,128)(2,1)S(1)} %get-tuple-element.22.pg0_ref, ...), custom_call_target="tpu_custom_call" | custom-call | flops 603979776 | bytes 3670016 | tf_op jit(solution)/shard_map/pallas_call | solution.py:302
  23.8 0.1 slice_bitcast_fusion
  23.8 2.2 %collective-permute-start.2 = (bf16[3584,128]{1,0:T(8,128)(2,1)S(1)}, bf16[3584,128]{1,0:T(8,128)(2,1)S(1)}, u32[]{:S(2)}, u32[]{:S(2)}) collective-permute-start(bf16[3584,128]{1,0:T(8,128)(2,1)S(1)} %slice_bitcast_fusion), channel_id=1, source_target_pairs={{0,1},{1,0},{16,17},{17,16},{8,9},{9,8},{24,25},{25,24},{2,3},{3,2... | collective-permute-start | bytes 2752520 | tf_op jit(solution)/shard_map/ppermute | solution.py:303
  26.0 2.1 %collective-permute-done.2 = bf16[3584,128]{1,0:T(8,128)(2,1)S(1)} collective-permute-done((bf16[3584,128]{1,0:T(8,128)(2,1)S(1)}, bf16[3584,128]{1,0:T(8,128)(2,1)S(1)}, u32[]{:S(2)}, u32[]{:S(2)}) %collective-permute-start.2) | collective-permute-done | bytes 917536 | tf_op jit(solution)/shard_map/ppermute | solution.py:303
  28.1 0.2 fusion
  28.4 23.1 %all_to_all.10 = bf16[32,112,128]{2,1,0:T(8,128)(2,1)S(1)} all-to-all(bf16[32,112,128]{2,1,0:T(8,128)(2,1)S(1)} %bitcast.19), channel_id=1, replica_groups={{0,16,8,24,2,18,10,26,32,48,40,56,34,50,42,58,64,80,72,88,66,82,74,90,9..., dimensions={0} | all-to-all | bytes 1835008 | tf_op jit(solution)/shard_map/all_to_all | solution.py:237
  51.5 0.0 copy-start.2
  51.5 0.1 convert_reduce_fusion
  51.6 2.0 %collective-permute-start.3 = (f32[112,128]{1,0:T(8,128)S(1)}, f32[112,128]{1,0:T(8,128)S(1)}, u32[]{:S(2)}, u32[]{:S(2)}) collective-permute-start(f32[112,128]{1,0:T(8,128)S(1)} %convert_reduce_fusion), channel_id=1, source_target_pairs={{0,6},{1,7},{16,22},{17,23},{8,14},{9,15},{24,30},{25,31},{2,4},{3... | collective-permute-start | bytes 172040 | tf_op jit(solution)/shard_map/ppermute | solution.py:321
  53.6 2.4 %collective-permute-done.3 = f32[112,128]{1,0:T(8,128)S(1)} collective-permute-done((f32[112,128]{1,0:T(8,128)S(1)}, f32[112,128]{1,0:T(8,128)S(1)}, u32[]{:S(2)}, u32[]{:S(2)}) %collective-permute-start.3) | collective-permute-done | bytes 57376 | tf_op jit(solution)/shard_map/ppermute | solution.py:321
  56.0 0.1 broadcast_in_dim.2
  56.1 15.5 %all_to_all.11 = bf16[32,112,128]{2,1,0:T(8,128)(2,1)S(1)} all-to-all(bf16[32,112,128]{2,1,0:T(8,128)(2,1)S(1)} %broadcast_in_dim.2), channel_id=1, replica_groups={{0,16,8,24,2,18,10,26,32,48,40,56,34,50,42,58,64,80,72,88,66,82,74,90,9..., dimensions={0} | all-to-all | bytes 1835008 | tf_op jit(solution)/shard_map/all_to_all | solution.py:237
  71.6 5.1 %collective-permute-start.4 = (bf16[3584,128]{1,0:T(8,128)(2,1)S(1)}, bf16[3584,128]{1,0:T(8,128)(2,1)S(1)}, u32[]{:S(2)}, u32[]{:S(2)}) collective-permute-start(bf16[3584,128]{1,0:T(8,128)(2,1)S(1)} %bitcast.14), channel_id=1, source_target_pairs={{0,1},{1,0},{16,17},{17,16},{8,9},{9,8},{24,25},{25,24},{2,3},{3,2... | collective-permute-start | bytes 2752520 | tf_op jit(solution)/shard_map/ppermute | solution.py:324
  76.8 0.0 copy-done.2
  76.8 5.3 %shard_map.78 = bf16[1,4,32,64,128]{4,3,2,1,0:T(8,128)(2,1)} custom-call(bf16[3,1152,256]{2,1,0:T(8,128)(2,1)S(1)} %copy-done.2, bf16[512,256]{1,0:T(8,128)(2,1)S(1)} %get-tuple-element.22.pg0_ref, bf16[512,256]{1,0:T(8,128)(2,1)S(1)} %get-tuple-element.23.pg1_ref, bf16[512,256]{1,0:T(8,128)(2,1)S(1)} %collective-permute-done.1.pn_ref), custom_call_target="tpu_custom_call" | custom-call | flops 2415919104 | bytes 4194304 | tf_op jit(solution)/shard_map/pallas_call | solution.py:306
  82.1 1.3 %own.1.held_ref = f32[3456,256]{1,0:T(8,128)} custom-call(s32[1]{0:T(128)} %bitcast.2.core_ref, bf16[3584,128]{1,0:T(8,128)(2,1)S(1)} %bitcast.15), custom_call_target="tpu_custom_call" | custom-call | flops 1048576 | bytes 3145728 | tf_op jit(solution)/shard_map/own/pallas_call | solution.py:246
  83.3 0.0 collective-permute-done.4.other_ref
  83.3 1.8 %other.1 = (f32[3456,256]{1,0:T(8,128)}, f32[1,256]{1,0:T(1,128)}) custom-call(s32[1]{0:T(128)} %bitcast.2.core_ref, bf16[3584,128]{1,0:T(8,128)(2,1)S(1)} %bitcast.16, bf16[3584,128]{1,0:T(8,128)(2,1)S(1)} %collective-permute-done.4.other_ref, f32[3456,256]{1,0:T(8,128)} %own.1.held_ref), custom_call_target="tpu_custom_call", output_to_operand_aliasing={{0}: (3, {})} | custom-call | flops 1048576 | bytes 3145728 | tf_op jit(solution)/shard_map/other/pallas_call | solution.py:256
  (1 shorter events, 0.0 us)
Async XLA Ops:
  0.6 7.0 %copy-start = (bf16[1,2,16,32,256]{4,3,2,1,0:T(8,128)(2,1)S(1)}, bf16[1,2,16,32,256]{4,3,2,1,0:T(8,128)(2,1)}, u32[]{:S(2)}) copy-start(bf16[1,2,16,32,256]{4,3,2,1,0:T(8,128)(2,1)} %g_ref.3) | copy-start | bytes 1572868
  0.6 7.0 %copy-start.3 = (f32[256]{0:T(256)S(1)}, f32[256]{0:T(256)}, u32[]{:S(2)}) copy-start(f32[256]{0:T(256)} %param.6) | copy-start | bytes 3076
  3.3 6.8 %copy-start.1 = (bf16[3,1152,256]{2,1,0:T(8,128)(2,1)}, bf16[3,1152,256]{2,1,0:T(8,128)(2,1)S(1)}, u32[]{:S(2)}) copy-start(bf16[3,1152,256]{2,1,0:T(8,128)(2,1)S(1)} %get-tuple-element.17.w_ref) | copy-start | bytes 5308420
  3.3 9.3 %collective-permute-start = (bf16[512,256]{1,0:T(8,128)(2,1)S(1)}, bf16[512,256]{1,0:T(8,128)(2,1)S(1)}, u32[]{:S(2)}, u32[]{:S(2)}) collective-permute-start(bf16[512,256]{1,0:T(8,128)(2,1)S(1)} %get-tuple-element.19), channel_id=1, source_target_pairs={{0,16},{16,32},{32,48},{48,64},{64,80},{80,96},{96,112},{1,17},{17... | collective-permute-start | bytes 786440 | tf_op jit(solution)/shard_map/ppermute | solution.py:233
  13.5 9.2 %collective-permute-start.1 = (bf16[512,256]{1,0:T(8,128)(2,1)S(1)}, bf16[512,256]{1,0:T(8,128)(2,1)S(1)}, u32[]{:S(2)}, u32[]{:S(2)}) collective-permute-start(bf16[512,256]{1,0:T(8,128)(2,1)S(1)} %get-tuple-element.22.pg0_ref), channel_id=1, source_target_pairs={{16,0},{32,16},{48,32},{64,48},{80,64},{96,80},{112,96},{17,1},{33... | collective-permute-start | bytes 786440 | tf_op jit(solution)/shard_map/ppermute | solution.py:233
  23.8 4.3 %collective-permute-start.2 = (bf16[3584,128]{1,0:T(8,128)(2,1)S(1)}, bf16[3584,128]{1,0:T(8,128)(2,1)S(1)}, u32[]{:S(2)}, u32[]{:S(2)}) collective-permute-start(bf16[3584,128]{1,0:T(8,128)(2,1)S(1)} %slice_bitcast_fusion), channel_id=1, source_target_pairs={{0,1},{1,0},{16,17},{17,16},{8,9},{9,8},{24,25},{25,24},{2,3},{3,2... | collective-permute-start | bytes 2752520 | tf_op jit(solution)/shard_map/ppermute | solution.py:303
  51.5 25.3 %copy-start.2 = (bf16[3,1152,256]{2,1,0:T(8,128)(2,1)S(1)}, bf16[3,1152,256]{2,1,0:T(8,128)(2,1)}, u32[]{:S(2)}) copy-start(bf16[3,1152,256]{2,1,0:T(8,128)(2,1)} %copy-done.1) | copy-start | bytes 5308420
  51.6 4.3 %collective-permute-start.3 = (f32[112,128]{1,0:T(8,128)S(1)}, f32[112,128]{1,0:T(8,128)S(1)}, u32[]{:S(2)}, u32[]{:S(2)}) collective-permute-start(f32[112,128]{1,0:T(8,128)S(1)} %convert_reduce_fusion), channel_id=1, source_target_pairs={{0,6},{1,7},{16,22},{17,23},{8,14},{9,15},{24,30},{25,31},{2,4},{3... | collective-permute-start | bytes 172040 | tf_op jit(solution)/shard_map/ppermute | solution.py:321
  71.6 11.7 %collective-permute-start.4 = (bf16[3584,128]{1,0:T(8,128)(2,1)S(1)}, bf16[3584,128]{1,0:T(8,128)(2,1)S(1)}, u32[]{:S(2)}, u32[]{:S(2)}) collective-permute-start(bf16[3584,128]{1,0:T(8,128)(2,1)S(1)} %bitcast.14), channel_id=1, source_target_pairs={{0,1},{1,0},{16,17},{17,16},{8,9},{9,8},{24,25},{25,24},{2,3},{3,2... | collective-permute-start | bytes 2752520 | tf_op jit(solution)/shard_map/ppermute | solution.py:324
